TPU v7x, 256 devices: a whole 4x4x8 slice. The times are simulated.
256 devices in a mesh: blk: 16 (over z, y_lo), img: 16 (over x, y_hi, core).
Axes of the slice: x: 4, y: 4 (y_hi: 2, y_lo: 2; y = y_hi * 2 + y_lo), z: 8, core: 2. Of those that a mesh axis runs over, the one named last changes fastest.
Arguments:
- hidden: bfloat16 [16, 2048, 1536], P('img', 'blk'), may hold values from -6 to 6
- text_hidden: bfloat16 [16, 154, 1536], P('img'), may hold values from -6 to 6
- latent: float32 [16, 64, 2048], P('img', 'blk'), may hold values from -6 to 6
- image_mod: float32 [16, 6, 1536], P('img'), may hold values from -10 to 10
- text_mod: float32 [16, 2, 1536], P('img'), may hold values from -3 to 3
- final_mod: float32 [16, 2, 1536], P('img'), may hold values from -3 to 3
- counts: int32 [16], P('img'), may hold values from 512 to 2048, as said below
- step_index: int32 [16], P('img'), may hold values from 0 to 7
- qkv_weight: bfloat16 [1536, 2304], P(None, 'img'), may hold values from -0.21875 to 0.21875
- text_weight: bfloat16 [1536, 1536], replicated, may hold values from -0.21875 to 0.21875
- out_weight: bfloat16 [768, 1536], replicated, may hold values from -0.21875 to 0.21875
- mlp_in_weight: bfloat16 [1536, 3072], P(None, 'img'), may hold values from -0.15625 to 0.15625
- mlp_out_weight: bfloat16 [3072, 1536], P(None, 'img'), may hold values from -0.109375 to 0.109375
- final_weight: bfloat16 [1536, 64], replicated, may hold values from -0.15625 to 0.15625
- conv_weight: bfloat16 [144, 512], replicated, may hold values from -0.5 to 0.5
- conv_bias: float32 [512], replicated, may hold values from -3 to 3
Outputs:
- velocity: float32 [16, 64, 2048], P('img', 'blk')
- next_latent: float32 [16, 64, 2048], P('img', 'blk')
- features: bfloat16 [16, 64, 128, 512], P('img', 'blk')
Inputs may be any that keep to these rules, and one draw needn't show every extreme that they name: `counts`: each count is a multiple of 128; in every draw one image has all 2048 patches.
All inputs are finite; a program needn't handle non-finite values.
Results may differ from a plain program's by a relative error of at most 0.015.
The roundings to bfloat16 on the way count: a program that leaves them out, or rounds other values in their place, can miss the bound.
Values may be sent and summed in bfloat16 or wider, within the bound.
No kernel may reach another device: no remote copies, remote signals or barrier semaphores. Data moves between devices by JAX's collectives and lax.ppermute only.
A program may use at most 128 MiB of HBM per device.

v0:
```python
import jax
import jax.numpy as jnp
from jax import lax
from jax.sharding import PartitionSpec as P

HEAD = 64
CH = 16
HEADS = 12
W_P = 64
STEPS = 8
norm_eps = 1e-06
sigma_shift = 3.0
vae_scale = 1.5305
vae_offset = 0.0609
masked_score = -1e30


def padded(x, sides, width):
    for axis, dim in sides:
        size, length = (lax.axis_size(axis), x.shape[dim])
        up = [(i, (i + 1) % size) for i in range(size - 1)]
        down = [(j, i) for i, j in up]
        last = lax.slice_in_dim(x, length - width, length, axis=dim)
        first = lax.slice_in_dim(x, 0, width, axis=dim)
        before = lax.ppermute(last, axis, up)
        after = lax.ppermute(first, axis, down)
        x = jnp.concatenate([before, x, after], axis=dim)
    return x


def modulate(inputs, shift_row, scale_row):
    values = inputs.astype(jnp.float32)
    center = jnp.mean(values, axis=-1, keepdims=True)
    spread = jnp.mean(jnp.square(values - center), axis=-1, keepdims=True)
    normed = (values - center) * lax.rsqrt(spread + norm_eps)
    return (normed * (1.0 + scale_row) + shift_row).astype(jnp.bfloat16)


def plan(step_value):
    remain = 1.0 - step_value / STEPS
    return sigma_shift * remain / (1.0 + (sigma_shift - 1.0) * remain)


def absorb(running, queries, key_rows, value_rows, key_valid):
    run_max, run_sum, run_out = running
    key_heads = key_rows.reshape(key_rows.shape[0], HEADS, HEAD)
    value_heads = value_rows.reshape(value_rows.shape[0], HEADS, HEAD)
    scores = (
        jnp.einsum("qhd,khd->hqk", queries, key_heads, preferred_element_type=jnp.float32) * 0.125
    )
    scores = jnp.where(key_valid[None, None, :], scores, masked_score)
    new_max = jnp.maximum(run_max, jnp.max(scores, axis=-1))
    factor = jnp.exp(run_max - new_max)
    numer = jnp.exp(scores - new_max[:, :, None])
    run_sum = run_sum * factor + jnp.sum(numer, axis=-1)
    run_out = run_out * factor[:, :, None] + jnp.einsum(
        "hqk,khd->hqd", numer.astype(jnp.bfloat16), value_heads, preferred_element_type=jnp.float32
    )
    return (new_max, run_sum, run_out)


def per_device(
    hidden,
    text_hidden,
    latent,
    image_mod,
    text_mod,
    final_mod,
    counts,
    step_index,
    qkv_weight,
    text_weight,
    out_weight,
    mlp_in_weight,
    mlp_out_weight,
    final_weight,
    conv_weight,
    conv_bias,
):
    tok_rows = hidden.shape[1]
    width_attn = HEADS * HEAD
    patch_count = counts[0]
    image_terms = image_mod[0]
    image_in = modulate(hidden[0], image_terms[0], image_terms[1])
    text_in = modulate(text_hidden[0], text_mod[0, 0], text_mod[0, 1])
    text_kv = jnp.dot(text_in, text_weight, preferred_element_type=jnp.float32).astype(jnp.bfloat16)
    qkv_all = jnp.dot(
        image_in,
        lax.all_gather(qkv_weight, "img", axis=1, tiled=True),
        preferred_element_type=jnp.float32,
    ).astype(jnp.bfloat16)
    queries = qkv_all[:, :width_attn].reshape(tok_rows, HEADS, HEAD)
    own_keys = qkv_all[:, width_attn : 2 * width_attn]
    own_values = qkv_all[:, 2 * width_attn :]
    start_state = (
        jnp.full((HEADS, tok_rows), -jnp.inf, jnp.float32),
        jnp.zeros((HEADS, tok_rows), jnp.float32),
        jnp.zeros((HEADS, tok_rows, HEAD), jnp.float32),
    )
    text_valid = jnp.ones((text_kv.shape[0],), dtype=bool)
    text_state = absorb(
        start_state, queries, text_kv[:, :width_attn], text_kv[:, width_attn:], text_valid
    )
    folded = text_state
    key_rows = lax.all_gather(own_keys, "blk", axis=0, tiled=True)
    value_rows = lax.all_gather(own_values, "blk", axis=0, tiled=True)
    blocks = key_rows.shape[0] // tok_rows
    key_blocks = key_rows.reshape(blocks, tok_rows, width_attn)
    value_blocks = value_rows.reshape(blocks, tok_rows, width_attn)

    def visit(running, block_item):
        key_block, value_block, block_pos = block_item
        block_first = block_pos * tok_rows
        key_valid = block_first + jnp.arange(tok_rows, dtype=jnp.int32) < patch_count
        running = absorb(running, queries, key_block, value_block, key_valid)
        return (running, None)

    folded, _ = lax.scan(
        visit, folded, (key_blocks, value_blocks, jnp.arange(blocks, dtype=jnp.int32))
    )
    run_max, run_sum, run_out = folded
    attended = (
        (run_out / run_sum[:, :, None])
        .transpose(1, 0, 2)
        .reshape(tok_rows, width_attn)
        .astype(jnp.bfloat16)
    )
    projected = jnp.dot(attended, out_weight, preferred_element_type=jnp.float32)
    updated = hidden[0].astype(jnp.float32) + image_terms[2] * projected
    mlp_in = modulate(updated, image_terms[3], image_terms[4])
    mlp_hidden = jax.nn.gelu(
        jnp.dot(
            mlp_in,
            lax.all_gather(mlp_in_weight, "img", axis=1, tiled=True),
            preferred_element_type=jnp.float32,
        ),
        approximate=True,
    ).astype(jnp.bfloat16)
    mlp_out = jnp.dot(
        mlp_hidden,
        lax.all_gather(mlp_out_weight, "img", axis=1, tiled=True),
        preferred_element_type=jnp.float32,
    )
    refined = updated + image_terms[5] * mlp_out
    final_in = modulate(refined, final_mod[0, 0], final_mod[0, 1])
    predicted = jnp.dot(final_in, final_weight, preferred_element_type=jnp.float32)
    patch_rows = tok_rows // W_P
    lat_rows = 2 * patch_rows
    vel_lat = (
        predicted.reshape(patch_rows, W_P, 2, 2, CH)
        .transpose(0, 2, 1, 3, 4)
        .reshape(lat_rows, 2 * W_P * CH)
    )
    global_rows = lax.axis_index("blk") * lat_rows + jnp.arange(lat_rows, dtype=jnp.int32)
    live_rows = (global_rows < 2 * (patch_count // W_P))[:, None]
    velocity = jnp.where(live_rows, vel_lat, 0.0)
    step_value = step_index[0].astype(jnp.float32)
    sigma_gap = plan(step_value + 1.0) - plan(step_value)
    next_lat = jnp.where(live_rows, latent[0] + sigma_gap * vel_lat, 0.0)
    scaled = jnp.where(live_rows, next_lat / vae_scale + vae_offset, 0.0).astype(jnp.bfloat16)
    framed = padded(scaled, (("blk", 0),), 1)
    padded_grid = jnp.pad(framed.reshape(lat_rows + 2, 2 * W_P, CH), ((0, 0), (1, 1), (0, 0)))
    columns = jnp.concatenate(
        [
            padded_grid[row_off : row_off + lat_rows, col_off : col_off + 2 * W_P, :]
            for row_off in range(3)
            for col_off in range(3)
        ],
        axis=-1,
    ).reshape(lat_rows * 2 * W_P, 9 * CH)
    feature = jnp.dot(columns, conv_weight, preferred_element_type=jnp.float32) + conv_bias
    feature = jnp.where(live_rows[:, :, None], feature.reshape(lat_rows, 2 * W_P, -1), 0.0).astype(
        jnp.bfloat16
    )
    return (velocity[None], next_lat[None], feature[None])


def solution(mesh):
    placed = (
        P("img", "blk", None),
        P("img", None, None),
        P("img", "blk", None),
        P("img", None, None),
        P("img", None, None),
        P("img", None, None),
        P("img"),
        P("img"),
        P(None, "img"),
        P(),
        P(),
        P(None, "img"),
        P(None, "img"),
        P(),
        P(),
        P(),
    )
    return jax.shard_map(
        per_device,
        mesh=mesh,
        in_specs=placed,
        out_specs=(P("img", "blk", None), P("img", "blk", None), P("img", "blk", None, None)),
        check_vma=False,
    )
```

profile of v0, /device:TPU:104, one launch (start us, length us, event | category | flops | bytes accessed | tf_op | source)
XLA Modules:
  0.0 461.3 jit_solution(7038986041568204380)
XLA Ops:
  8.0 1.3 fusion.64
  9.3 1.4 slice_reduce_fusion.2
  13.1 71.2 %all-gather.6.cloned.1.call-done = bf16[1536,2304]{0,1:T(8,128)(2,1)} async-done(((bf16[1536,144]{0,1:T(8,128)(2,1)}), bf16[1536,2304]{0,1:T(8,128)(2,1)}) %all-gather.6.cloned.1.call-update) | async-done | bytes 7077904 | tf_op jit(solution)/shard_map/all_gather | solution.py:89
  84.3 5.6 %convolution_convert_fusion = bf16[128,2304]{1,0:T(8,128)(2,1)S(1)} fusion(bf16[1536,2304]{0,1:T(8,128)(2,1)} %all-gather.6.cloned.1.call-done, bf16[1,128,1536]{2,1,0:T(8,128)(2,1)} %param.18, f32[1536]{0:T(1024)S(1)} %get-tuple-element.72, f32[1536]{0:T(1024)S(1)} %get-tuple-element.76, f32[128]{0:T(128)S(1)} %add_rsqrt_fusion.3, ...), kind=kOutput, calls=%fused_computation.13 | convolution fusion | flops 907444224 | bytes 8074240 | tf_op jit(solution)/shard_map/dot_general | solution.py:87
  93.8 3.3 convolution_convert_fusion.1
  100.4 1.8 copy.32
  102.2 1.3 fusion.75
  105.3 64.7 %all-gather.8.cloned.1.call-done = bf16[2048,768]{1,0:T(8,128)(2,1)} async-done(((bf16[128,768]{1,0:T(8,128)(2,1)}), bf16[2048,768]{1,0:T(8,128)(2,1)}) %all-gather.8.cloned.1.call-update) | async-done | bytes 3145744 | tf_op jit(solution)/shard_map/all_gather | solution.py:105
  170.0 81.6 %all-gather.10.cloned.1.call-done = bf16[2048,768]{1,0:T(8,128)(2,1)} async-done(((bf16[128,768]{1,0:T(8,128)(2,1)}), bf16[2048,768]{1,0:T(8,128)(2,1)}) %all-gather.10.cloned.1.call-update) | async-done | bytes 3145744 | tf_op jit(solution)/shard_map/all_gather | solution.py:106
  252.1 138.2 %while.14 = (s32[]{:T(128)}, f32[12,128]{1,0:T(8,128)S(1)}, f32[12,128]{1,0:T(8,128)}, f32[12,128,64]{1,2,0:T(8,128)}, s32[16]{0:T(128)}, /*index=5*/s32[]{:T(12...) while((s32[]{:T(128)}, f32[12,128]{1,0:T(8,128)S(1)}, ...), condition=%wide.region_9.10_spmd, body=%wide.region_6.9_spmd.sunk | while | flops 51907840 | bytes 5407121 | solution.py:118
  257.3 1.3 multiply_add_fusion.2
  258.7 2.0 convolution_add_fusion.4
  264.5 1.3 fusion.103
  265.9 1.3 multiply_add_fusion.2
  267.3 2.0 convolution_add_fusion.4
  274.5 1.3 multiply_add_fusion.2
  276.0 2.0 convolution_add_fusion.4
  283.1 1.3 multiply_add_fusion.2
  284.6 2.0 convolution_add_fusion.4
  290.3 1.3 fusion.103
  291.7 1.3 multiply_add_fusion.2
  293.2 2.0 convolution_add_fusion.4
  299.0 1.3 fusion.103
  300.4 1.3 multiply_add_fusion.2
  301.9 2.0 convolution_add_fusion.4
  309.1 1.3 multiply_add_fusion.2
  310.5 2.0 convolution_add_fusion.4
  316.3 1.3 fusion.103
  317.7 1.3 multiply_add_fusion.2
  319.2 2.0 convolution_add_fusion.4
  324.9 1.3 fusion.103
  326.3 1.3 multiply_add_fusion.2
  327.8 2.0 convolution_add_fusion.4
  333.5 1.3 fusion.103
  335.0 1.3 multiply_add_fusion.2
  336.5 2.0 convolution_add_fusion.4
  342.2 1.3 fusion.103
  343.6 1.3 multiply_add_fusion.2
  345.1 2.0 convolution_add_fusion.4
  350.8 1.3 fusion.103
  352.3 1.3 multiply_add_fusion.2
  353.7 2.0 convolution_add_fusion.4
  359.5 1.3 fusion.103
  360.9 1.3 multiply_add_fusion.2
  362.3 2.0 convolution_add_fusion.4
  368.1 1.3 fusion.103
  369.5 1.3 multiply_add_fusion.2
  371.0 2.0 convolution_add_fusion.4
  376.7 1.4 fusion.103
  378.2 1.3 multiply_add_fusion.2
  379.7 2.0 convolution_add_fusion.4
  385.4 1.3 fusion.103
  386.8 1.3 multiply_add_fusion.2
  388.3 2.0 convolution_add_fusion.4
  391.4 1.6 fusion.76
  393.3 25.1 %all-gather.14.cloned.1.call-done = bf16[3072,1536]{0,1:T(8,128)(2,1)} async-done(((bf16[3072,96]{0,1:T(8,128)(2,1)}), bf16[3072,1536]{0,1:T(8,128)(2,1)}) %all-gather.14.cloned.1.call-update) | async-done | bytes 9437200 | tf_op jit(solution)/shard_map/all_gather | solution.py:141
  418.4 13.7 %fusion.77 = (f32[128]{0:T(128)S(1)}, f32[128,1536]{1,0:T(8,128)}) fusion(f32[128,1536]{1,0:T(8,128)S(1)} %get-tuple-element.127, bf16[3072,1536]{0,1:T(8,128)(2,1)} %all-gather.14.cloned.1.call-done, bf16[1536,3072]{0,1:T(8,128)(2,1)} %all-gather.12.cloned.1.call-done, f32[1536]{0:T(1024)S(1)} %copy-done.9, f32[1536]{0:T(1024)S(1)} %copy-done.7, ...), kind=kOutput, calls=%fused_computation.130 | convolution fusion | flops 2421030912 | bytes 20467200 | tf_op jit(solution)/shard_map/dot_general | solution.py:139
  432.1 1.4 multiply_reduce_fusion
  433.6 1.5 fusion.58
  435.9 5.6 %collective-permute-start = (bf16[1,2048]{1,0:T(2,128)(2,1)S(1)}, bf16[1,2048]{1,0:T(2,128)(2,1)S(1)}, u32[]{:S(2)}, u32[]{:S(2)}) collective-permute-start(bf16[1,2048]{1,0:T(2,128)(2,1)S(1)} %get-tuple-element.120), channel_id=1, source_target_pairs={{0,16},{16,32},{32,48},{48,64},{64,80},{80,96},{96,112},{112,128},... | collective-permute-start | bytes 12296 | tf_op jit(solution)/shard_map/ppermute | solution.py:25
  441.5 1.9 collective-permute-start.1
  445.2 3.9 collective-permute-done.1
  450.5 2.0 concatenate.40
  452.5 1.3 convolution_add_fusion.1
  (221 shorter events, 76.6 us)
Async XLA Ops:
  7.2 384.2 %copy-start = (bf16[768,1536]{1,0:T(8,128)(2,1)S(1)}, bf16[768,1536]{1,0:T(8,128)(2,1)}, u32[]{:S(2)}) copy-start(bf16[768,1536]{1,0:T(8,128)(2,1)} %param.28) | copy-start | bytes 7077892
  7.2 77.1 %all-gather.6.cloned.1.call-start = ((), (), s32[]{:S(2)}) async-start(), calls=%async_computation | async-start | bytes 7520256 | tf_op jit(solution)/shard_map/all_gather | solution.py:89
  7.9 162.1 %all-gather.8.cloned.1.call-start = ((), (), s32[]{:S(2)}) async-start(), calls=%async_computation.1 | async-start | bytes 3342336 | tf_op jit(solution)/shard_map/all_gather | solution.py:105
  84.3 9.0 %copy-start.5 = (f32[1,2,1536]{2,1,0:T(2,128)S(1)}, f32[1,2,1536]{2,1,0:T(2,128)}, u32[]{:S(2)}) copy-start(f32[1,2,1536]{2,1,0:T(2,128)} %param.22) | copy-start | bytes 36868
  89.9 3.5 copy-start.1
  90.7 160.9 %all-gather.10.cloned.1.call-start = ((), (), s32[]{:S(2)}) async-start(), calls=%async_computation.2 | async-start | bytes 3342336 | tf_op jit(solution)/shard_map/all_gather | solution.py:106
  91.5 301.8 %all-gather.12.cloned.1.call-start = ((), (), s32[]{:S(2)}) async-start(), calls=%async_computation.3 | async-start | bytes 10027008 | tf_op jit(solution)/shard_map/all_gather | solution.py:134
  92.1 326.3 %all-gather.14.cloned.1.call-start = ((), (), s32[]{:S(2)}) async-start(), calls=%async_computation.4 | async-start | bytes 10027008 | tf_op jit(solution)/shard_map/all_gather | solution.py:141
  93.8 3.8 copy-start.6
  93.8 5.6 %copy-start.3 = (f32[1,4,2048]{2,1,0:T(4,128)S(1)}, f32[1,4,2048]{2,1,0:T(4,128)}, u32[]{:S(2)}) copy-start(f32[1,4,2048]{2,1,0:T(4,128)} %param.20) | copy-start | bytes 98308
  98.9 153.2 %copy-start.12 = (pred[4]{0:T(512)(128)(4,1)}, pred[4]{0:T(512)(128)(4,1)S(1)}, u32[]{:S(2)}) copy-start(pred[4]{0:T(512)(128)(4,1)S(1)} %add_compare_fusion.1) | copy-start | bytes 16
  390.3 28.1 %copy-start.7 = (f32[1536]{0:T(1024)S(1)}, f32[1536]{0:T(1024)}, u32[]{:S(2)}) copy-start(f32[1536]{0:T(1024)} %get-tuple-element.75) | copy-start | bytes 18436
  390.3 28.1 %copy-start.8 = (f32[1536]{0:T(1024)S(1)}, f32[1536]{0:T(1024)}, u32[]{:S(2)}) copy-start(f32[1536]{0:T(1024)} %get-tuple-element.71) | copy-start | bytes 18436
  390.3 28.1 %copy-start.9 = (f32[1536]{0:T(1024)S(1)}, f32[1536]{0:T(1024)}, u32[]{:S(2)}) copy-start(f32[1536]{0:T(1024)} %get-tuple-element.74) | copy-start | bytes 18436
  418.4 15.2 %copy-start.10 = (f32[1536]{0:T(1024)S(1)}, f32[1536]{0:T(1024)}, u32[]{:S(2)}) copy-start(f32[1536]{0:T(1024)} %get-tuple-element.77) | copy-start | bytes 18436
  418.4 15.2 %copy-start.11 = (f32[1536]{0:T(1024)S(1)}, f32[1536]{0:T(1024)}, u32[]{:S(2)}) copy-start(f32[1536]{0:T(1024)} %get-tuple-element.78) | copy-start | bytes 18436
  418.4 15.2 %copy-start.15 = (bf16[1536,64]{0,1:T(8,128)(2,1)S(1)}, bf16[1536,64]{0,1:T(8,128)(2,1)}, u32[]{:S(2)}) copy-start(bf16[1536,64]{0,1:T(8,128)(2,1)} %param.31) | copy-start | bytes 589828
  418.4 17.4 %copy-start.4 = (f32[1,4,2048]{2,1,0:T(4,128)S(1)}, f32[1,4,2048]{2,1,0:T(4,128)}, u32[]{:S(2)}) copy-start(f32[1,4,2048]{2,1,0:T(4,128)} %param.20) | copy-start | bytes 98308
  418.4 17.4 %copy-start.13 = (pred[4]{0:T(512)(128)(4,1)S(1)}, pred[4]{0:T(512)(128)(4,1)}, u32[]{:S(2)}) copy-start(pred[4]{0:T(512)(128)(4,1)} %copy-done.12) | copy-start | bytes 16
  432.1 12.3 %copy-start.2 = (f32[512,16]{1,0:T(8,128)S(1)}, f32[512,16]{1,0:T(8,128)}, u32[]{:S(2)}) copy-start(f32[512,16]{1,0:T(8,128)} %squeeze.13) | copy-start | bytes 98308
  432.1 12.3 %copy-start.14 = (pred[512]{0:T(512)(128)(4,1)S(1)}, pred[512]{0:T(512)(128)(4,1)}, u32[]{:S(2)}) copy-start(pred[512]{0:T(512)(128)(4,1)} %broadcast_bitcast_fusion) | copy-start | bytes 1540
  433.6 18.9 %copy-start.16 = (f32[512]{0:T(512)S(1)}, f32[512]{0:T(512)}, u32[]{:S(2)}) copy-start(f32[512]{0:T(512)} %param.33) | copy-start | bytes 6148
  435.9 9.3 %collective-permute-start = (bf16[1,2048]{1,0:T(2,128)(2,1)S(1)}, bf16[1,2048]{1,0:T(2,128)(2,1)S(1)}, u32[]{:S(2)}, u32[]{:S(2)}) collective-permute-start(bf16[1,2048]{1,0:T(2,128)(2,1)S(1)} %get-tuple-element.120), channel_id=1, source_target_pairs={{0,16},{16,32},{32,48},{48,64},{64,80},{80,96},{96,112},{112,128},... | collective-permute-start | bytes 12296 | tf_op jit(solution)/shard_map/ppermute | solution.py:25
  441.5 7.7 %collective-permute-start.1 = (bf16[1,2048]{1,0:T(2,128)(2,1)S(1)}, bf16[1,2048]{1,0:T(2,128)(2,1)S(1)}, u32[]{:S(2)}, u32[]{:S(2)}) collective-permute-start(bf16[1,2048]{1,0:T(2,128)(2,1)S(1)} %get-tuple-element.121), channel_id=1, source_target_pairs={{16,0},{32,16},{48,32},{64,48},{80,64},{96,80},{112,96},{128,112},... | collective-permute-start | bytes 12296 | tf_op jit(solution)/shard_map/ppermute | solution.py:26
Sparse Core Ops, SparseCore 0:
  10.7 73.5 all-gather.5
  90.9 79.1 all-gather.7
  171.8 79.7 all-gather.9
  254.2 81.4 all-gather.11
  338.2 80.0 all-gather.13
where the time goes:
time: 464 us; the launch traced here: 461 us
  waiting for transfers between devices  249 us (54%)
  matrix products  81.7 us (18%)
  local copies, waits for them, and re-layouts  52.2 us (11%)
  other arithmetic  44.4 us (10%)
  between operations  15.6 us (3%)
  loops' own time  10.9 us (2%)
  starting transfers between devices  7.67 us (2%)
    all_gather x1, waiting for transfers between devices, per_device(): value_rows = lax.all_gather(own_values, 'blk', axis=0, tiled=True)  81.6 us
    all_gather x1, waiting for transfers between devices, per_device(): lax.all_gather(qkv_weight, 'img', axis=1, tiled=True)  71.2 us
    all_gather x1, waiting for transfers between devices, per_device(): key_rows = lax.all_gather(own_keys, 'blk', axis=0, tiled=True)  64.7 us
    dynamic_slice x64, local copies, waits for them, and re-layouts, per_device(): lax.scan(visit, folded, (key_blocks, value_blocks, jnp.arange(blocks, dty...  41.5 us
    dot_general x17, matrix products, absorb(): jnp.einsum('hqk,khd->hqd', numer.astype(jnp.bfloat16), value_heads, prefe...  33.1 us
    all_gather x1, waiting for transfers between devices, per_device(): lax.all_gather(mlp_out_weight, 'img', axis=1, tiled=True)  25.1 us
    dot_general x17, matrix products, absorb(): jnp.einsum('qhd,khd->hqk', queries, key_heads, preferred_element_type=jnp...  21.6 us
    add x16, other arithmetic, absorb(): run_sum = run_sum * factor + jnp.sum(numer, axis=-1)  20.8 us
  transfers between devices with their start and end apart: 7, of which 5 were waited for; matrix products, arithmetic and copies ran while one was open for 32% of the time, Pallas kernels for 0%

commit v1 on v0

--- a/solution.py
+++ b/solution.py
@@ -138,7 +138,9 @@
     ).astype(jnp.bfloat16)
     mlp_out = jnp.dot(
         mlp_hidden,
-        lax.all_gather(mlp_out_weight, "img", axis=1, tiled=True),
+        jnp.concatenate(
+            lax.all_to_all(jnp.stack([mlp_out_weight] * lax.axis_size("img")), "img", 0, 0), axis=1
+        ),
         preferred_element_type=jnp.float32,
     )
     refined = updated + image_terms[5] * mlp_out

time: 464 us -> 537 us (1.16)
  waiting for transfers between devices: 249 us -> 313 us
  local copies, waits for them, and re-layouts: 52.2 us -> 57.6 us
    all_gather x1, waiting for transfers between devices: 64.7 us -> 155 us  [per_device(): key_rows = lax.all_gather(own_keys, 'blk', axis=0, tiled=True)]
    all_gather x1 -> x0, waiting for transfers between devices: 25.1 us -> none  [per_device(): lax.all_gather(mlp_out_weight, 'img', axis=1, tiled=True)]
  transfers between devices with their start and end apart: 7 -> 7, of which waited for: 5 -> 4; matrix products, arithmetic and copies ran while one was open for 32% -> 29% of each run, Pallas kernels for 0% -> 0%
where the time goes in v1:
time: 537 us; the launch traced here: 534 us
  waiting for transfers between devices  313 us (58%)
  matrix products  81.5 us (15%)
  local copies, waits for them, and re-layouts  57.6 us (11%)
  other arithmetic  44.5 us (8%)
  between operations  15.6 us (3%)
  starting transfers between devices  11.1 us (2%)
  loops' own time  10.7 us (2%)
    all_gather x1, waiting for transfers between devices, per_device(): key_rows = lax.all_gather(own_keys, 'blk', axis=0, tiled=True)  155 us
    all_gather x1, waiting for transfers between devices, per_device(): value_rows = lax.all_gather(own_values, 'blk', axis=0, tiled=True)  82 us
    all_gather x1, waiting for transfers between devices, per_device(): lax.all_gather(qkv_weight, 'img', axis=1, tiled=True)  71.2 us
    dynamic_slice x64, local copies, waits for them, and re-layouts, per_device(): lax.scan(visit, folded, (key_blocks, value_blocks, jnp.arange(blocks, dty...  42 us
    dot_general x17, matrix products, absorb(): jnp.einsum('hqk,khd->hqd', numer.astype(jnp.bfloat16), value_heads, prefe...  33 us
    dot_general x17, matrix products, absorb(): jnp.einsum('qhd,khd->hqk', queries, key_heads, preferred_element_type=jnp...  21.5 us
    add x16, other arithmetic, absorb(): run_sum = run_sum * factor + jnp.sum(numer, axis=-1)  20.9 us
    dot_general x1, matrix products, per_device(): jnp.dot(mlp_hidden, jnp.concatenate(lax.all_to_all(jnp.stack([mlp_out_wei...  13.7 us
  transfers between devices with their start and end apart: 7, of which 4 were waited for; matrix products, arithmetic and copies ran while one was open for 29% of the time, Pallas kernels for 0%

profile of v1, /device:TPU:104, one launch (start us, length us, event | category | flops | bytes accessed | tf_op | source)
XLA Modules:
  0.0 534.3 jit_solution(10384403005119726184)
XLA Ops:
  8.0 1.3 fusion.64
  9.3 1.4 slice_reduce_fusion.2
  13.1 71.2 %all-gather.5.cloned.1.call-done = bf16[1536,2304]{0,1:T(8,128)(2,1)} async-done(((bf16[1536,144]{0,1:T(8,128)(2,1)}), bf16[1536,2304]{0,1:T(8,128)(2,1)}) %all-gather.5.cloned.1.call-update) | async-done | bytes 7077904 | tf_op jit(solution)/shard_map/all_gather | solution.py:89
  84.3 5.6 %convolution_convert_fusion = bf16[128,2304]{1,0:T(8,128)(2,1)S(1)} fusion(bf16[1536,2304]{0,1:T(8,128)(2,1)} %all-gather.5.cloned.1.call-done, bf16[1,128,1536]{2,1,0:T(8,128)(2,1)} %param.18, f32[1536]{0:T(1024)S(1)} %get-tuple-element.72, f32[1536]{0:T(1024)S(1)} %get-tuple-element.76, f32[128]{0:T(128)S(1)} %add_rsqrt_fusion.3, ...), kind=kOutput, calls=%fused_computation.13 | convolution fusion | flops 907444224 | bytes 8074240 | tf_op jit(solution)/shard_map/dot_general | solution.py:87
  91.5 4.9 stack.2
  96.4 4.9 all-to-all-start
  103.1 3.3 convolution_convert_fusion.1
  109.8 1.8 copy.33
  111.5 1.3 fusion.75
  114.6 154.5 %all-gather.7.cloned.1.call-done = bf16[2048,768]{1,0:T(8,128)(2,1)} async-done(((bf16[128,768]{1,0:T(8,128)(2,1)}), bf16[2048,768]{1,0:T(8,128)(2,1)}) %all-gather.7.cloned.1.call-update) | async-done | bytes 3145744 | tf_op jit(solution)/shard_map/all_gather | solution.py:105
  269.2 82.0 %all-gather.9.cloned.1.call-done = bf16[2048,768]{1,0:T(8,128)(2,1)} async-done(((bf16[128,768]{1,0:T(8,128)(2,1)}), bf16[2048,768]{1,0:T(8,128)(2,1)}) %all-gather.9.cloned.1.call-update) | async-done | bytes 3145744 | tf_op jit(solution)/shard_map/all_gather | solution.py:106
  351.7 138.3 %while.14 = (s32[]{:T(128)}, f32[12,128]{1,0:T(8,128)S(1)}, f32[12,128]{1,0:T(8,128)}, f32[12,128,64]{1,2,0:T(8,128)}, s32[16]{0:T(128)}, /*index=5*/s32[]{:T(12...) while((s32[]{:T(128)}, f32[12,128]{1,0:T(8,128)S(1)}, ...), condition=%wide.region_9.10_spmd, body=%wide.region_6.9_spmd.sunk | while | flops 51907840 | bytes 5407121 | solution.py:118
  355.5 1.3 fusion.103
  356.9 1.3 multiply_add_fusion.2
  358.4 2.0 convolution_add_fusion.4
  365.5 1.3 multiply_add_fusion.2
  367.0 2.0 convolution_add_fusion.4
  372.8 1.3 fusion.103
  374.2 1.3 multiply_add_fusion.2
  375.6 2.0 convolution_add_fusion.4
  381.4 1.3 fusion.103
  382.8 1.3 multiply_add_fusion.2
  384.3 2.0 convolution_add_fusion.4
  390.0 1.3 fusion.103
  391.5 1.3 multiply_add_fusion.2
  392.9 2.0 convolution_add_fusion.4
  398.7 1.3 fusion.103
  400.1 1.3 multiply_add_fusion.2
  401.6 2.0 convolution_add_fusion.4
  408.8 1.3 multiply_add_fusion.2
  410.3 2.0 convolution_add_fusion.4
  416.1 1.3 fusion.103
  417.5 1.3 multiply_add_fusion.2
  418.9 2.0 convolution_add_fusion.4
  424.7 1.3 fusion.103
  426.1 1.3 multiply_add_fusion.2
  427.6 2.0 convolution_add_fusion.4
  433.3 1.3 fusion.103
  434.8 1.3 multiply_add_fusion.2
  436.2 2.0 convolution_add_fusion.4
  442.0 1.3 fusion.103
  443.4 1.3 multiply_add_fusion.2
  444.9 2.0 convolution_add_fusion.4
  452.0 1.3 multiply_add_fusion.2
  453.5 2.0 convolution_add_fusion.4
  459.3 1.3 fusion.103
  460.7 1.3 multiply_add_fusion.2
  462.1 2.0 convolution_add_fusion.4
  469.3 1.3 multiply_add_fusion.2
  470.8 2.0 convolution_add_fusion.4
  476.5 1.3 fusion.103
  477.9 1.3 multiply_add_fusion.2
  479.4 2.0 convolution_add_fusion.4
  486.6 1.3 multiply_add_fusion.2
  488.0 2.0 convolution_add_fusion.4
  491.1 1.6 fusion.76
  493.1 13.7 %fusion.77 = (f32[128]{0:T(128)S(1)}, f32[128,1536]{1,0:T(8,128)}) fusion(f32[128,1536]{1,0:T(8,128)S(1)} %get-tuple-element.127, bf16[3072,1536]{0,1:T(8,128)(2,1)} %bitcast.15, bf16[1536,3072]{0,1:T(8,128)(2,1)} %all-gather.11.cloned.1.call-done, f32[1536]{0:T(1024)S(1)} %copy-done.10, f32[1536]{0:T(1024)S(1)} %copy-done.8, f32[128]{0:T(128)S(1)} %add_rsqrt_fusion.2, ...), kind=kOutput, calls=%fused_computation.130 | convolution fusion | flops 2421030912 | bytes 20467200 | tf_op jit(solution)/shard_map/dot_general | solution.py:139
  506.8 1.4 multiply_reduce_fusion
  508.3 1.5 fusion.58
  510.6 3.8 collective-permute-start
  514.4 2.0 collective-permute-start.1
  518.3 3.8 collective-permute-done.1
  523.4 2.0 concatenate.40
  525.5 1.3 convolution_add_fusion.1
  (223 shorter events, 77.8 us)
Async XLA Ops:
  7.2 484.0 %copy-start = (bf16[768,1536]{1,0:T(8,128)(2,1)S(1)}, bf16[768,1536]{1,0:T(8,128)(2,1)}, u32[]{:S(2)}) copy-start(bf16[768,1536]{1,0:T(8,128)(2,1)} %param.28) | copy-start | bytes 7077892
  7.2 77.1 %all-gather.5.cloned.1.call-start = ((), (), s32[]{:S(2)}) async-start(), calls=%async_computation.1 | async-start | bytes 7520256 | tf_op jit(solution)/shard_map/all_gather | solution.py:89
  7.9 261.3 %all-gather.7.cloned.1.call-start = ((), (), s32[]{:S(2)}) async-start(), calls=%async_computation.2 | async-start | bytes 3342336 | tf_op jit(solution)/shard_map/all_gather | solution.py:105
  84.3 7.2 %copy-start.3 = (bf16[3072,96]{0,1:T(8,128)(2,1)S(1)}, bf16[3072,96]{0,1:T(8,128)(2,1)}, u32[]{:S(2)}) copy-start(bf16[3072,96]{0,1:T(8,128)(2,1)} %param.30) | copy-start | bytes 1769476
  90.8 260.5 %all-gather.9.cloned.1.call-start = ((), (), s32[]{:S(2)}) async-start(), calls=%async_computation.3 | async-start | bytes 3342336 | tf_op jit(solution)/shard_map/all_gather | solution.py:106
  96.4 6.2 %copy-start.6 = (f32[1,2,1536]{2,1,0:T(2,128)S(1)}, f32[1,2,1536]{2,1,0:T(2,128)}, u32[]{:S(2)}) copy-start(f32[1,2,1536]{2,1,0:T(2,128)} %param.22) | copy-start | bytes 36868
  96.4 6.2 %copy-start.1 = (bf16[1,154,1536]{2,1,0:T(8,128)(2,1)S(1)}, bf16[1,154,1536]{2,1,0:T(8,128)(2,1)}, u32[]{:S(2)}) copy-start(bf16[1,154,1536]{2,1,0:T(8,128)(2,1)} %param.19) | copy-start | bytes 1419268
  96.4 396.6 %all-to-all-start = ((bf16[16,3072,96]{1,2,0:T(8,128)(2,1)}), bf16[16,3072,96]{1,2,0:T(8,128)(2,1)}, u32[]{:S(2)}, u32[]{:S(2)}) async-start(bf16[16,3072,96]{1,2,0:T(8,128)(2,1)} %stack.2), calls=%async_computation | async-start | bytes 18874368 | tf_op jit(solution)/shard_map/all_to_all | solution.py:142
  101.3 391.7 %all-gather.11.cloned.1.call-start = ((), (), s32[]{:S(2)}) async-start(), calls=%async_computation.4 | async-start | bytes 10027008 | tf_op jit(solution)/shard_map/all_gather | solution.py:134
  103.1 3.8 copy-start.7
  103.1 5.7 %copy-start.4 = (f32[1,4,2048]{2,1,0:T(4,128)S(1)}, f32[1,4,2048]{2,1,0:T(4,128)}, u32[]{:S(2)}) copy-start(f32[1,4,2048]{2,1,0:T(4,128)} %param.20) | copy-start | bytes 98308
  108.2 243.5 %copy-start.13 = (pred[4]{0:T(512)(128)(4,1)}, pred[4]{0:T(512)(128)(4,1)S(1)}, u32[]{:S(2)}) copy-start(pred[4]{0:T(512)(128)(4,1)S(1)} %add_compare_fusion.1) | copy-start | bytes 16
  490.0 3.0 copy-start.8
  490.0 3.0 copy-start.9
  490.0 3.0 copy-start.10
  493.1 15.2 %copy-start.11 = (f32[1536]{0:T(1024)S(1)}, f32[1536]{0:T(1024)}, u32[]{:S(2)}) copy-start(f32[1536]{0:T(1024)} %get-tuple-element.77) | copy-start | bytes 18436
  493.1 15.2 %copy-start.12 = (f32[1536]{0:T(1024)S(1)}, f32[1536]{0:T(1024)}, u32[]{:S(2)}) copy-start(f32[1536]{0:T(1024)} %get-tuple-element.78) | copy-start | bytes 18436
  493.1 15.2 %copy-start.16 = (bf16[1536,64]{0,1:T(8,128)(2,1)S(1)}, bf16[1536,64]{0,1:T(8,128)(2,1)}, u32[]{:S(2)}) copy-start(bf16[1536,64]{0,1:T(8,128)(2,1)} %param.31) | copy-start | bytes 589828
  493.1 17.4 %copy-start.5 = (f32[1,4,2048]{2,1,0:T(4,128)S(1)}, f32[1,4,2048]{2,1,0:T(4,128)}, u32[]{:S(2)}) copy-start(f32[1,4,2048]{2,1,0:T(4,128)} %param.20) | copy-start | bytes 98308
  493.1 17.4 %copy-start.14 = (pred[4]{0:T(512)(128)(4,1)S(1)}, pred[4]{0:T(512)(128)(4,1)}, u32[]{:S(2)}) copy-start(pred[4]{0:T(512)(128)(4,1)} %copy-done.13) | copy-start | bytes 16
  506.8 10.7 %copy-start.2 = (f32[512,16]{1,0:T(8,128)S(1)}, f32[512,16]{1,0:T(8,128)}, u32[]{:S(2)}) copy-start(f32[512,16]{1,0:T(8,128)} %squeeze.13) | copy-start | bytes 98308
  506.8 10.7 %copy-start.15 = (pred[512]{0:T(512)(128)(4,1)S(1)}, pred[512]{0:T(512)(128)(4,1)}, u32[]{:S(2)}) copy-start(pred[512]{0:T(512)(128)(4,1)} %broadcast_bitcast_fusion) | copy-start | bytes 1540
  508.3 17.2 %copy-start.17 = (f32[512]{0:T(512)S(1)}, f32[512]{0:T(512)}, u32[]{:S(2)}) copy-start(f32[512]{0:T(512)} %param.33) | copy-start | bytes 6148
  510.6 7.7 %collective-permute-start = (bf16[1,2048]{1,0:T(2,128)(2,1)S(1)}, bf16[1,2048]{1,0:T(2,128)(2,1)S(1)}, u32[]{:S(2)}, u32[]{:S(2)}) collective-permute-start(bf16[1,2048]{1,0:T(2,128)(2,1)S(1)} %get-tuple-element.120), channel_id=1, source_target_pairs={{0,16},{16,32},{32,48},{48,64},{64,80},{80,96},{96,112},{112,128},... | collective-permute-start | bytes 12296 | tf_op jit(solution)/shard_map/ppermute | solution.py:25
  514.4 7.7 %collective-permute-start.1 = (bf16[1,2048]{1,0:T(2,128)(2,1)S(1)}, bf16[1,2048]{1,0:T(2,128)(2,1)S(1)}, u32[]{:S(2)}, u32[]{:S(2)}) collective-permute-start(bf16[1,2048]{1,0:T(2,128)(2,1)S(1)} %get-tuple-element.121), channel_id=1, source_target_pairs={{16,0},{32,16},{48,32},{64,48},{80,64},{96,80},{112,96},{128,112},... | collective-permute-start | bytes 12296 | tf_op jit(solution)/shard_map/ppermute | solution.py:26
Sparse Core Ops, SparseCore 0:
  10.7 73.5 all-gather.4
  90.9 178.2 all-gather.6
  271.0 80.2 all-gather.8
  353.8 81.4 all-gather.10
